TPU v7x, 32 devices: a whole 2x2x4 slice. The times are simulated.
32 devices in a mesh: grp: 2 (over x), tm: 4 (over y, core), tile: 4 (over z).
Axes of the slice: x: 2, y: 2, z: 4, core: 2. Of those that a mesh axis runs over, the one named last changes fastest.
Arguments:
- frames: bfloat16 [64, 1024, 1024], P(('grp', 'tm'), 'tile'), parts along dimension 0, may hold values from -3 to 3
- inverse_taps: float32 [48], replicated, may hold values from -3 to 3
- mode_rate: float32 [1024, 1024], P(None, 'tile'), may hold values from 0.00625 to 0.2
- frame_factor: float32 [64], P(('grp', 'tm')), parts along dimension 0, may hold values from 0.5 to 1
Outputs:
- superheat: bfloat16 [64, 1024, 1024], P(('grp', 'tm'), 'tile'), parts along dimension 0
There are 2 independent parts, one for each index of `grp`. A program takes and returns all parts, laid end to end along the dimension named above; an argument that names none is the same for every part. Nothing has to cross between parts.
All inputs are finite; a program needn't handle non-finite values.
Results may differ from a plain program's by a relative error of at most 0.0097.
Values may be sent and summed in bfloat16 or wider, within the bound.
A program may use at most 128 MiB of HBM per device.

v0:
```python
import jax
import jax.numpy as jnp
from jax import lax
from jax.sharding import PartitionSpec as P


def from_behind(block, axis, distance):
    devices = range(lax.axis_size(axis))
    route = [(i - distance, i) for i in devices if i - distance in devices]
    return lax.ppermute(block, axis, route)


def cosine_matrix(points):
    freq_idx = jnp.arange(points, dtype=jnp.int32)[:, None]
    cell_idx = jnp.arange(points, dtype=jnp.int32)[None, :]
    phase = (2 * cell_idx + 1) * freq_idx % (4 * points)
    angle = jnp.pi * phase.astype(jnp.float32) / (2.0 * points)
    values = jnp.cos(angle) * jnp.sqrt(2.0 / points)
    values = jnp.where(freq_idx == 0, values / jnp.sqrt(2.0), values)
    return values.astype(jnp.bfloat16)


def on_device(frames, inverse_taps, mode_rate, frame_factor):
    segment_span, tile_rows, frame_side = frames.shape
    tap_count = inverse_taps.shape[0]
    basis = cosine_matrix(frame_side)
    taps_b = inverse_taps.astype(jnp.bfloat16).astype(jnp.float32)
    offset = (
        jnp.arange(segment_span)[:, None]
        + (tap_count - 1)
        - jnp.arange(segment_span + tap_count - 1)[None, :]
    )
    onehot = offset[:, :, None] == jnp.arange(tap_count)[None, None, :]
    toeplitz = jnp.sum(jnp.where(onehot, taps_b[None, None, :], 0.0), axis=2).astype(jnp.bfloat16)
    reach = (tap_count - 1 + segment_span - 1) // segment_span
    hop_count = min(reach, lax.axis_size("tm") - 1)
    received = []
    moving = frames
    for hop_index in range(hop_count):
        moving = from_behind(moving, "tm", 1)
        received.append(moving)
    missing = reach - hop_count
    pieces = []
    if missing > 0:
        pieces.append(jnp.zeros((missing * segment_span, tile_rows, frame_side), jnp.bfloat16))
    pieces = pieces + received[::-1]
    history_all = jnp.concatenate(pieces, axis=0)
    earlier = history_all[history_all.shape[0] - (tap_count - 1) :]
    joined = jnp.concatenate([earlier, frames], axis=0)
    wall_heat_flux = jnp.einsum("tj,jrw->trw", toeplitz, joined, preferred_element_type=jnp.float32)
    wall_heat_flux = wall_heat_flux.astype(jnp.bfloat16)
    spectra = jnp.einsum(
        "kr,frc->fkc",
        basis,
        lax.all_to_all(
            jnp.einsum(
                "frw,kw->frk", wall_heat_flux, basis, preferred_element_type=jnp.float32
            ).astype(jnp.bfloat16),
            "tile",
            split_axis=2,
            concat_axis=1,
            tiled=True,
        ),
        preferred_element_type=jnp.float32,
    )
    retain = jnp.exp(-mode_rate)

    def advance(held, inputs):
        decay, running = held
        spectrum, factor = inputs
        rate_now = retain * factor
        decay = rate_now * decay
        running = rate_now * running + spectrum
        return ((decay, running), (decay, running))

    start_decay = jnp.ones_like(retain)
    start_state = jnp.zeros_like(retain)
    (last_decay, last_state), (decays, partial_value) = lax.scan(
        advance, (start_decay, start_state), (spectra, frame_factor)
    )

    def turn(round_number, incoming):
        return from_behind(last_decay * incoming + last_state, "tm", 1)

    carried = lax.fori_loop(0, lax.axis_size("tm") - 1, turn, start_state)
    running_b = (partial_value + decays * carried[None]).astype(jnp.bfloat16)
    return jnp.einsum(
        "frk,kw->frw",
        lax.all_to_all(
            jnp.einsum("kr,fkc->frc", basis, running_b, preferred_element_type=jnp.float32).astype(
                jnp.bfloat16
            ),
            "tile",
            split_axis=1,
            concat_axis=2,
            tiled=True,
        ),
        basis,
        preferred_element_type=jnp.float32,
    ).astype(jnp.bfloat16)


def solution(mesh):
    return jax.shard_map(
        on_device,
        mesh=mesh,
        in_specs=(P(("grp", "tm"), "tile", None), P(), P(None, "tile"), P(("grp", "tm"))),
        out_specs=P(("grp", "tm"), "tile", None),
        check_vma=False,
    )
```

profile of v0, /device:TPU:1, one launch (start us, length us, event | category | flops | bytes accessed | tf_op | source)
XLA Modules:
  0.0 596.6 jit_solution(18411087734227628912)
XLA Ops:
  4.5 4.5 collective-permute-start.1
  9.1 45.4 %collective-permute-done.1 = bf16[8,256,1024]{2,0,1:T(8,128)(2,1)S(1)} collective-permute-done((bf16[8,256,1024]{2,0,1:T(8,128)(2,1)S(1)}, bf16[8,256,1024]{2,0,1:T(8,128)(2,1)S(1)}, u32[]{:S(2)}, u32[]{:S(2)}) %collective-permute-start.1) | collective-permute-done | bytes 4194336 | tf_op jit(solution)/shard_map/ppermute | solution.py:10
  58.9 45.4 %collective-permute-done.2 = bf16[8,256,1024]{2,0,1:T(8,128)(2,1)S(1)} collective-permute-done((bf16[8,256,1024]{2,0,1:T(8,128)(2,1)S(1)}, bf16[8,256,1024]{2,0,1:T(8,128)(2,1)S(1)}, u32[]{:S(2)}, u32[]{:S(2)}) %collective-permute-start.2) | collective-permute-done | bytes 4194336 | tf_op jit(solution)/shard_map/ppermute | solution.py:10
  109.0 45.1 %collective-permute-done.3 = bf16[8,256,1024]{2,0,1:T(8,128)(2,1)S(1)} collective-permute-done((bf16[8,256,1024]{2,0,1:T(8,128)(2,1)S(1)}, bf16[8,256,1024]{2,0,1:T(8,128)(2,1)S(1)}, u32[]{:S(2)}, u32[]{:S(2)}) %collective-permute-start.3) | collective-permute-done | bytes 4194336 | tf_op jit(solution)/shard_map/ppermute | solution.py:10
  154.1 14.9 %pad_maximum_fusion = bf16[47,256,1024]{2,0,1:T(8,128)(2,1)} fusion(bf16[8,256,1024]{2,0,1:T(8,128)(2,1)S(1)} %collective-permute-done.1, bf16[8,256,1024]{2,0,1:T(8,128)(2,1)S(1)} %collective-permute-done.2, bf16[8,256,1024]{2,0,1:T(8,128)(2,1)S(1)} %collective-permute-done.3, bf16[47]{0:T(256)(128)(2,1)S(1)} %pad_slice_fusion), kind=kLoop, calls=%fused_computation.11 | loop fusion | flops 98566144 | bytes 37224544 | tf_op jit(solution)/shard_map/concatenate | solution.py:47
  169.0 14.9 %fusion.18 = bf16[8,256,1024]{2,0,1:T(8,128)(2,1)} fusion(bf16[8,256,1024]{2,0,1:T(8,128)(2,1)} %copy-done, bf16[47,256,1024]{2,0,1:T(8,128)(2,1)} %pad_maximum_fusion, bf16[8,55]{1,0:T(8,128)(2,1)S(1)} %select_reduce_fusion), kind=kOutput, calls=%fused_computation.35 | convolution fusion | flops 290455552 | bytes 33031024 | tf_op jit(solution)/shard_map/tj,jrw->trw/dot_general | solution.py:50
  183.9 30.2 %fusion.15 = bf16[8,256,1024]{2,1,0:T(8,128)(2,1)} fusion(bf16[8,256,1024]{2,0,1:T(8,128)(2,1)} %fusion.18, s32[1024]{0:T(1024)S(1)} %multiply_add_fusion.1, pred[1024]{0:T(1024)(128)(4,1)S(1)} %iota_compare_fusion.1), kind=kOutput, calls=%fused_computation.34 | convolution fusion | flops 4315938816 | bytes 8393728 | tf_op jit(solution)/shard_map/frw,kw->frk/dot_general | solution.py:56
  214.1 7.0 %copy.18 = bf16[8,256,1024]{1,0,2:T(8,128)(2,1)} copy(bf16[8,256,1024]{2,1,0:T(8,128)(2,1)} %fusion.15) | data formatting | bytes 8388608 | tf_op jit(solution)/shard_map/convert_element_type | solution.py:58
  221.1 5.0 all-to-all-start
  227.4 52.1 %all-to-all-done = bf16[8,256,1024]{1,0,2:T(8,128)(2,1)} async-done(((bf16[8,256,1024]{1,0,2:T(8,128)(2,1)}), bf16[8,256,1024]{1,0,2:T(8,128)(2,1)}, u32[]{:S(2)}, u32[]{:S(2)}) %all-to-all-start) | async-done | bytes 4194336 | tf_op jit(solution)/shard_map/all_to_all | solution.py:55
  279.5 7.4 %copy.33 = bf16[8,256,4,256]{1,2,3,0:T(4,128)(2,1)} copy(bf16[8,256,4,256]{1,0,3,2:T(8,128)(2,1)} %bitcast.2) | data formatting | bytes 8388608 | tf_op jit(solution)/shard_map/all_to_all | solution.py:55
  286.9 7.8 %all_to_all.29 = bf16[8,1024,256]{1,2,0:T(8,128)(2,1)} reshape(bf16[8,4,256,256]{2,1,3,0:T(4,128)(2,1)} %bitcast.37) | data formatting | bytes 8388608 | tf_op jit(solution)/shard_map/all_to_all | solution.py:55
  294.7 23.9 %convolution_bitcast_fusion = f32[8,1024,256]{1,2,0:T(8,128)} fusion(bf16[8,1024,256]{1,2,0:T(8,128)(2,1)} %all_to_all.29, s32[1024]{0:T(1024)S(1)} %multiply_add_fusion.1, pred[1024]{0:T(1024)(128)(4,1)S(1)} %iota_compare_fusion.1), kind=kOutput, calls=%fused_computation.33 | convolution fusion | flops 4313841664 | bytes 12588032 | tf_op jit(solution)/shard_map/kr,frc->fkc/dot_general | solution.py:52
  318.6 69.1 %while.28 = (s32[]{:T(128)}, f32[1024,256]{1,0:T(8,128)S(1)}, f32[1024,256]{1,0:T(8,128)S(1)}, f32[8,1024,256]{2,1,0:T(8,128)}, f32[8,1024,256]{2,1,0:T(8,128)},...) while((s32[]{:T(128)}, f32[1024,256]{1,0:T(8,128)S(1)}, ...), condition=%wide.region_2.3_spmd.clone, body=%wide.region_1.2_spmd.clone.sunk | while | flops 1572867 | bytes 12584063 | solution.py:78
  387.7 52.3 %while.27 = (s32[]{:T(128)}, f32[1024,256]{1,0:T(8,128)S(1)}, f32[1024,256]{1,0:T(8,128)S(1)}, f32[1024,256]{1,0:T(8,128)S(1)}, s32[]{:T(128)}) while((s32[]{:T(128)}, f32[1024,256]{1,0:T(8,128)S(1)}, f32[1024,256]{1,0:T(8,128)S(1)}, f32[1024,256]{1,0:T(8,128)S(1)}, s32[]{:T(128)}) %tuple.47), condition=%wide.region_4.5_spmd, body=%wide.region_3.4_spmd.sunk | while | flops 524290 | bytes 8388709 | solution.py:85
  392.8 12.0 %collective-permute-done = f32[1024,256]{1,0:T(8,128)S(1)} collective-permute-done((f32[1024,256]{1,0:T(8,128)}, f32[1024,256]{1,0:T(8,128)S(1)}, u32[]{:S(2)}, u32[]{:S(2)}) %collective-permute-start) | collective-permute-done | bytes 1048608 | tf_op jit(solution)/shard_map/while/body/eval_jaxpr/ppermute | solution.py:10
  410.3 12.0 %collective-permute-done = f32[1024,256]{1,0:T(8,128)S(1)} collective-permute-done((f32[1024,256]{1,0:T(8,128)}, f32[1024,256]{1,0:T(8,128)S(1)}, u32[]{:S(2)}, u32[]{:S(2)}) %collective-permute-start) | collective-permute-done | bytes 1048608 | tf_op jit(solution)/shard_map/while/body/eval_jaxpr/ppermute | solution.py:10
  427.8 12.0 %collective-permute-done = f32[1024,256]{1,0:T(8,128)S(1)} collective-permute-done((f32[1024,256]{1,0:T(8,128)}, f32[1024,256]{1,0:T(8,128)S(1)}, u32[]{:S(2)}, u32[]{:S(2)}) %collective-permute-start) | collective-permute-done | bytes 1048608 | tf_op jit(solution)/shard_map/while/body/eval_jaxpr/ppermute | solution.py:10
  440.0 27.7 %convert_bitcast_fusion = bf16[8,1024,256]{1,2,0:T(8,128)(2,1)} fusion(f32[8,1024,256]{2,1,0:T(8,128)} %get-tuple-element.72, f32[8,1024,256]{2,1,0:T(8,128)} %get-tuple-element.73, f32[1024,256]{1,0:T(8,128)S(1)} %get-tuple-element.76, s32[1024]{0:T(1024)S(1)} %multiply_add_fusion.1, pred[1024]{0:T(1024)(128)(4,1)S(1)} %iota_compare_fusion.1), kind=kOutput, calls=%fused_computation.27 | convolution fusion | flops 4322230272 | bytes 22025216 | tf_op jit(solution)/shard_map/kr,fkc->frc/dot_general | solution.py:90
  467.6 6.9 %copy.22 = bf16[8,1024,256]{2,0,1:T(8,128)(2,1)} copy(bf16[8,1024,256]{1,2,0:T(8,128)(2,1)} %convert_bitcast_fusion) | data formatting | bytes 8388608 | tf_op jit(solution)/shard_map/convert_element_type | solution.py:90
  474.6 86.2 %all_to_all.36 = bf16[8,1024,256]{2,0,1:T(8,128)(2,1)S(1)} all-to-all(bf16[8,1024,256]{2,0,1:T(8,128)(2,1)} %copy.22), channel_id=1, replica_groups=mesh['grp'=2,'tm'=4,'tile'=4] {'tile'}, dimensions={1} | all-to-all | bytes 8388608 | tf_op jit(solution)/shard_map/all_to_all | solution.py:89
  560.7 5.2 copy.32
  566.0 7.7 %all_to_all.33 = bf16[8,256,1024]{2,1,0:T(8,128)(2,1)} reshape(bf16[8,256,4,256]{3,2,1,0:T(4,128)(2,1)} %bitcast.39) | data formatting | bytes 8388608 | tf_op jit(solution)/shard_map/all_to_all | solution.py:89
  573.7 22.5 %convolution_convert_fusion = bf16[8,256,1024]{2,1,0:T(8,128)(2,1)} fusion(bf16[8,256,1024]{2,1,0:T(8,128)(2,1)} %all_to_all.33, s32[1024]{0:T(1024)S(1)} %multiply_add_fusion.1, pred[1024]{0:T(1024)(128)(4,1)S(1)} %iota_compare_fusion.1), kind=kOutput, calls=%fused_computation.36 | convolution fusion | flops 4315938816 | bytes 8393728 | tf_op jit(solution)/shard_map/frk,kw->frw/dot_general | solution.py:87
  (63 shorter events, 99.8 us)
Async XLA Ops:
  0.0 108.8 %copy-start.2 = (f32[48]{0:T(128)S(1)}, f32[48]{0:T(128)}, u32[]{:S(2)}) copy-start(f32[48]{0:T(128)} %param.9) | copy-start | bytes 580
  4.5 149.6 %copy-start = (bf16[8,256,1024]{2,0,1:T(8,128)(2,1)}, bf16[8,256,1024]{2,0,1:T(8,128)(2,1)S(1)}, u32[]{:S(2)}) copy-start(bf16[8,256,1024]{2,0,1:T(8,128)(2,1)S(1)} %copy.15) | copy-start | bytes 12582916
  4.5 50.0 %collective-permute-start.1 = (bf16[8,256,1024]{2,0,1:T(8,128)(2,1)S(1)}, bf16[8,256,1024]{2,0,1:T(8,128)(2,1)S(1)}, u32[]{:S(2)}, u32[]{:S(2)}) collective-permute-start(bf16[8,256,1024]{2,0,1:T(8,128)(2,1)S(1)} %copy.15), channel_id=1, source_target_pairs={{0,4},{4,8},{8,12},{1,5},{5,9},{9,13},{2,6},{6,10},{10,14},{3,7},{... | collective-permute-start | bytes 12582920 | tf_op jit(solution)/shard_map/ppermute | solution.py:10
  54.5 49.8 %collective-permute-start.2 = (bf16[8,256,1024]{2,0,1:T(8,128)(2,1)S(1)}, bf16[8,256,1024]{2,0,1:T(8,128)(2,1)S(1)}, u32[]{:S(2)}, u32[]{:S(2)}) collective-permute-start(bf16[8,256,1024]{2,0,1:T(8,128)(2,1)S(1)} %collective-permute-done.1), channel_id=1, source_target_pairs={{0,4},{4,8},{8,12},{1,5},{5,9},{9,13},{2,6},{6,10},{10,14},{3,7},{... | collective-permute-start | bytes 12582920 | tf_op jit(solution)/shard_map/ppermute | solution.py:10
  104.3 49.8 %collective-permute-start.3 = (bf16[8,256,1024]{2,0,1:T(8,128)(2,1)S(1)}, bf16[8,256,1024]{2,0,1:T(8,128)(2,1)S(1)}, u32[]{:S(2)}, u32[]{:S(2)}) collective-permute-start(bf16[8,256,1024]{2,0,1:T(8,128)(2,1)S(1)} %collective-permute-done.2), channel_id=1, source_target_pairs={{0,4},{4,8},{8,12},{1,5},{5,9},{9,13},{2,6},{6,10},{10,14},{3,7},{... | collective-permute-start | bytes 12582920 | tf_op jit(solution)/shard_map/ppermute | solution.py:10
  221.1 5.0 copy-start.1
  221.1 58.3 %all-to-all-start = ((bf16[8,256,1024]{1,0,2:T(8,128)(2,1)}), bf16[8,256,1024]{1,0,2:T(8,128)(2,1)}, u32[]{:S(2)}, u32[]{:S(2)}) async-start(bf16[8,256,1024]{1,0,2:T(8,128)(2,1)} %copy.18), calls=%async_computation | async-start | bytes 8388608 | tf_op jit(solution)/shard_map/all_to_all | solution.py:55
  294.7 23.9 %copy-start.3 = (f32[8]{0:T(128)S(1)}, f32[8]{0:T(128)}, u32[]{:S(2)}) copy-start(f32[8]{0:T(128)} %param.11) | copy-start | bytes 100
  388.9 15.9 %collective-permute-start = (f32[1024,256]{1,0:T(8,128)}, f32[1024,256]{1,0:T(8,128)S(1)}, u32[]{:S(2)}, u32[]{:S(2)}) collective-permute-start(f32[1024,256]{1,0:T(8,128)} %multiply_add_fusion.3), channel_id=1, source_target_pairs={{0,4},{4,8},{8,12},{1,5},{5,9},{9,13},{2,6},{6,10},{10,14},{3,7},{... | collective-permute-start | bytes 3145736 | tf_op jit(solution)/shard_map/while/body/eval_jaxpr/ppermute | solution.py:10
  406.0 16.3 %collective-permute-start = (f32[1024,256]{1,0:T(8,128)}, f32[1024,256]{1,0:T(8,128)S(1)}, u32[]{:S(2)}, u32[]{:S(2)}) collective-permute-start(f32[1024,256]{1,0:T(8,128)} %multiply_add_fusion.3), channel_id=1, source_target_pairs={{0,4},{4,8},{8,12},{1,5},{5,9},{9,13},{2,6},{6,10},{10,14},{3,7},{... | collective-permute-start | bytes 3145736 | tf_op jit(solution)/shard_map/while/body/eval_jaxpr/ppermute | solution.py:10
  423.5 16.3 %collective-permute-start = (f32[1024,256]{1,0:T(8,128)}, f32[1024,256]{1,0:T(8,128)S(1)}, u32[]{:S(2)}, u32[]{:S(2)}) collective-permute-start(f32[1024,256]{1,0:T(8,128)} %multiply_add_fusion.3), channel_id=1, source_target_pairs={{0,4},{4,8},{8,12},{1,5},{5,9},{9,13},{2,6},{6,10},{10,14},{3,7},{... | collective-permute-start | bytes 3145736 | tf_op jit(solution)/shard_map/while/body/eval_jaxpr/ppermute | solution.py:10
where the time goes:
time: 605 us; the launch traced here: 597 us
  waiting for transfers between devices  224 us (37%)
  matrix products  119 us (20%)
  blocking collectives  86.2 us (14%)
  local copies, waits for them, and re-layouts  82.4 us (14%)
  other arithmetic  53.2 us (9%)
  starting transfers between devices  30.7 us (5%)
    ppermute x6, waiting for transfers between devices, from_behind(): return lax.ppermute(block, axis, route)  172 us
    all_to_all x1, blocking collectives, on_device(): lax.all_to_all(jnp.einsum('kr,fkc->frc', basis, running_b, preferred_elem...  86.2 us
    all_to_all x1, waiting for transfers between devices, on_device(): lax.all_to_all(jnp.einsum('frw,kw->frk', wall_heat_flux, basis, preferred...  52.1 us
    dynamic_slice x24, local copies, waits for them, and re-layouts, on_device(): lax.scan(advance, (start_decay, start_state), (spectra, frame_factor))  35.6 us
    dynamic_update_slice x8, other arithmetic, on_device(): lax.scan(advance, (start_decay, start_state), (spectra, frame_factor))  33.4 us
    dot_general x1, matrix products, on_device(): jnp.einsum('frw,kw->frk', wall_heat_flux, basis, preferred_element_type=j...  30.2 us
    dot_general x1, matrix products, on_device(): jnp.einsum('kr,fkc->frc', basis, running_b, preferred_element_type=jnp.fl...  27.7 us
    ppermute x6, starting transfers between devices, from_behind(): return lax.ppermute(block, axis, route)  25.7 us
  transfers between devices with their start and end apart: 7, of which 7 were waited for; matrix products, arithmetic and copies ran while one was open for 0% of the time, Pallas kernels for 0%

commit v1 on v0

--- a/solution.py
+++ b/solution.py
@@ -2,6 +2,13 @@
 import jax.numpy as jnp
 from jax import lax
 from jax.sharding import PartitionSpec as P
+
+shape_members_all_on_mesh = lambda view: jnp.concatenate(
+    jax.lax.all_to_all(
+        jnp.stack(jnp.split(view, jax.lax.axis_size("tile"), axis=1), axis=0), "tile", 0, 0
+    ),
+    axis=2,
+)
 
 
 def from_behind(block, axis, distance):
@@ -86,14 +93,10 @@
     running_b = (partial_value + decays * carried[None]).astype(jnp.bfloat16)
     return jnp.einsum(
         "frk,kw->frw",
-        lax.all_to_all(
+        shape_members_all_on_mesh(
             jnp.einsum("kr,fkc->frc", basis, running_b, preferred_element_type=jnp.float32).astype(
                 jnp.bfloat16
-            ),
-            "tile",
-            split_axis=1,
-            concat_axis=2,
-            tiled=True,
+            )
         ),
         basis,
         preferred_element_type=jnp.float32,

time: 605 us -> 582 us (0.962)
  local copies, waits for them, and re-layouts: 82.4 us -> 63.4 us
    all_to_all x2 -> x0, local copies, waits for them, and re-layouts: 12.9 us -> none  [on_device(): lax.all_to_all(jnp.einsum('kr,fkc->frc', basis, running_b, preferred_elem...]
    convert_element_type x1 -> x0, local copies, waits for them, and re-layouts: 6.94 us -> none  [on_device(): jnp.einsum('kr,fkc->frc', basis, running_b, preferred_element_type=jnp.fl...]
where the time goes in v1:
time: 582 us; the launch traced here: 573 us
  waiting for transfers between devices  224 us (38%)
  matrix products  115 us (20%)
  blocking collectives  85.2 us (15%)
  local copies, waits for them, and re-layouts  63.4 us (11%)
  other arithmetic  53.8 us (9%)
  starting transfers between devices  30.7 us (5%)
    ppermute x6, waiting for transfers between devices, from_behind(): return lax.ppermute(block, axis, route)  172 us
    all_to_all x1, blocking collectives, jax.lax.all_to_all(jnp.stack(jnp.split(view, jax.lax.axis_size('tile'), a...  85.2 us
    all_to_all x1, waiting for transfers between devices, on_device(): lax.all_to_all(jnp.einsum('frw,kw->frk', wall_heat_flux, basis, preferred...  52.1 us
    dynamic_slice x24, local copies, waits for them, and re-layouts, on_device(): lax.scan(advance, (start_decay, start_state), (spectra, frame_factor))  35.6 us
    dynamic_update_slice x8, other arithmetic, on_device(): lax.scan(advance, (start_decay, start_state), (spectra, frame_factor))  33.4 us
    dot_general x1, matrix products, on_device(): jnp.einsum('frw,kw->frk', wall_heat_flux, basis, preferred_element_type=j...  30.2 us
    ppermute x6, starting transfers between devices, from_behind(): return lax.ppermute(block, axis, route)  25.7 us
    dot_general x1, matrix products, on_device(): jnp.einsum('kr,fkc->frc', basis, running_b, preferred_element_type=jnp.fl...  25.6 us
  transfers between devices with their start and end apart: 7, of which 7 were waited for; matrix products, arithmetic and copies ran while one was open for 0% of the time, Pallas kernels for 0%

profile of v1, /device:TPU:1, one launch (start us, length us, event | category | flops | bytes accessed | tf_op | source)
XLA Modules:
  0.0 573.5 jit_solution(5446612645143857947)
XLA Ops:
  0.0 4.5 copy.22
  4.5 4.5 collective-permute-start.1
  9.1 45.4 %collective-permute-done.1 = bf16[8,256,1024]{2,0,1:T(8,128)(2,1)S(1)} collective-permute-done((bf16[8,256,1024]{2,0,1:T(8,128)(2,1)S(1)}, bf16[8,256,1024]{2,0,1:T(8,128)(2,1)S(1)}, u32[]{:S(2)}, u32[]{:S(2)}) %collective-permute-start.1) | collective-permute-done | bytes 4194336 | tf_op jit(solution)/shard_map/ppermute | solution.py:17
  54.5 4.4 collective-permute-start.2
  58.9 45.4 %collective-permute-done.2 = bf16[8,256,1024]{2,0,1:T(8,128)(2,1)S(1)} collective-permute-done((bf16[8,256,1024]{2,0,1:T(8,128)(2,1)S(1)}, bf16[8,256,1024]{2,0,1:T(8,128)(2,1)S(1)}, u32[]{:S(2)}, u32[]{:S(2)}) %collective-permute-start.2) | collective-permute-done | bytes 4194336 | tf_op jit(solution)/shard_map/ppermute | solution.py:17
  104.3 4.4 collective-permute-start.3
  109.0 45.1 %collective-permute-done.3 = bf16[8,256,1024]{2,0,1:T(8,128)(2,1)S(1)} collective-permute-done((bf16[8,256,1024]{2,0,1:T(8,128)(2,1)S(1)}, bf16[8,256,1024]{2,0,1:T(8,128)(2,1)S(1)}, u32[]{:S(2)}, u32[]{:S(2)}) %collective-permute-start.3) | collective-permute-done | bytes 4194336 | tf_op jit(solution)/shard_map/ppermute | solution.py:17
  154.1 14.9 %pad_maximum_fusion = bf16[47,256,1024]{2,0,1:T(8,128)(2,1)} fusion(bf16[8,256,1024]{2,0,1:T(8,128)(2,1)S(1)} %collective-permute-done.1, bf16[8,256,1024]{2,0,1:T(8,128)(2,1)S(1)} %collective-permute-done.2, bf16[8,256,1024]{2,0,1:T(8,128)(2,1)S(1)} %collective-permute-done.3, bf16[47]{0:T(256)(128)(2,1)S(1)} %pad_slice_fusion), kind=kLoop, calls=%fused_computation.11 | loop fusion | flops 98566144 | bytes 37224544 | tf_op jit(solution)/shard_map/concatenate | solution.py:54
  169.0 14.9 %fusion.18 = bf16[8,256,1024]{2,0,1:T(8,128)(2,1)} fusion(bf16[8,256,1024]{2,0,1:T(8,128)(2,1)} %copy-done, bf16[47,256,1024]{2,0,1:T(8,128)(2,1)} %pad_maximum_fusion, bf16[8,55]{1,0:T(8,128)(2,1)S(1)} %select_reduce_fusion), kind=kOutput, calls=%fused_computation.35 | convolution fusion | flops 290455552 | bytes 33031024 | tf_op jit(solution)/shard_map/tj,jrw->trw/dot_general | solution.py:57
  183.9 30.2 %fusion.15 = bf16[8,256,1024]{2,1,0:T(8,128)(2,1)} fusion(bf16[8,256,1024]{2,0,1:T(8,128)(2,1)} %fusion.18, s32[1024]{0:T(1024)S(1)} %multiply_add_fusion.1, pred[1024]{0:T(1024)(128)(4,1)S(1)} %iota_compare_fusion.1), kind=kOutput, calls=%fused_computation.34 | convolution fusion | flops 4315938816 | bytes 8393728 | tf_op jit(solution)/shard_map/frw,kw->frk/dot_general | solution.py:63
  214.1 7.0 %copy.25 = bf16[8,256,1024]{1,0,2:T(8,128)(2,1)} copy(bf16[8,256,1024]{2,1,0:T(8,128)(2,1)} %fusion.15) | data formatting | bytes 8388608 | tf_op jit(solution)/shard_map/convert_element_type | solution.py:65
  221.1 5.0 all-to-all-start
  227.4 52.1 %all-to-all-done = bf16[8,256,1024]{1,0,2:T(8,128)(2,1)} async-done(((bf16[8,256,1024]{1,0,2:T(8,128)(2,1)}), bf16[8,256,1024]{1,0,2:T(8,128)(2,1)}, u32[]{:S(2)}, u32[]{:S(2)}) %all-to-all-start) | async-done | bytes 4194336 | tf_op jit(solution)/shard_map/all_to_all | solution.py:62
  279.5 7.4 %copy.39 = bf16[8,256,4,256]{1,2,3,0:T(4,128)(2,1)} copy(bf16[8,256,4,256]{1,0,3,2:T(8,128)(2,1)} %bitcast.2) | data formatting | bytes 8388608 | tf_op jit(solution)/shard_map/all_to_all | solution.py:62
  286.9 7.8 %all_to_all.19 = bf16[8,1024,256]{1,2,0:T(8,128)(2,1)} reshape(bf16[8,4,256,256]{2,1,3,0:T(4,128)(2,1)} %bitcast.43) | data formatting | bytes 8388608 | tf_op jit(solution)/shard_map/all_to_all | solution.py:62
  294.7 23.8 %convolution_bitcast_fusion = f32[8,1024,256]{1,2,0:T(8,128)} fusion(bf16[8,1024,256]{1,2,0:T(8,128)(2,1)} %all_to_all.19, s32[1024]{0:T(1024)S(1)} %multiply_add_fusion.1, pred[1024]{0:T(1024)(128)(4,1)S(1)} %iota_compare_fusion.1), kind=kOutput, calls=%fused_computation.33 | convolution fusion | flops 4313841664 | bytes 12588032 | tf_op jit(solution)/shard_map/kr,frc->fkc/dot_general | solution.py:59
  318.5 69.0 %while.28 = (s32[]{:T(128)}, f32[1024,256]{1,0:T(8,128)S(1)}, f32[1024,256]{1,0:T(8,128)S(1)}, f32[8,1024,256]{2,1,0:T(8,128)}, f32[8,1024,256]{2,1,0:T(8,128)},...) while((s32[]{:T(128)}, f32[1024,256]{1,0:T(8,128)S(1)}, ...), condition=%wide.region_2.3_spmd.clone, body=%wide.region_1.2_spmd.clone.sunk | while | flops 1572867 | bytes 12584063 | solution.py:85
  387.6 52.3 %while.27 = (s32[]{:T(128)}, f32[1024,256]{1,0:T(8,128)S(1)}, f32[1024,256]{1,0:T(8,128)S(1)}, f32[1024,256]{1,0:T(8,128)S(1)}, s32[]{:T(128)}) while((s32[]{:T(128)}, f32[1024,256]{1,0:T(8,128)S(1)}, f32[1024,256]{1,0:T(8,128)S(1)}, f32[1024,256]{1,0:T(8,128)S(1)}, s32[]{:T(128)}) %tuple.51), condition=%wide.region_4.5_spmd, body=%wide.region_3.4_spmd.sunk | while | flops 524290 | bytes 8388709 | solution.py:92
  392.7 12.0 %collective-permute-done = f32[1024,256]{1,0:T(8,128)S(1)} collective-permute-done((f32[1024,256]{1,0:T(8,128)}, f32[1024,256]{1,0:T(8,128)S(1)}, u32[]{:S(2)}, u32[]{:S(2)}) %collective-permute-start) | collective-permute-done | bytes 1048608 | tf_op jit(solution)/shard_map/while/body/eval_jaxpr/ppermute | solution.py:17
  410.2 12.0 %collective-permute-done = f32[1024,256]{1,0:T(8,128)S(1)} collective-permute-done((f32[1024,256]{1,0:T(8,128)}, f32[1024,256]{1,0:T(8,128)S(1)}, u32[]{:S(2)}, u32[]{:S(2)}) %collective-permute-start) | collective-permute-done | bytes 1048608 | tf_op jit(solution)/shard_map/while/body/eval_jaxpr/ppermute | solution.py:17
  427.7 12.0 %collective-permute-done = f32[1024,256]{1,0:T(8,128)S(1)} collective-permute-done((f32[1024,256]{1,0:T(8,128)}, f32[1024,256]{1,0:T(8,128)S(1)}, u32[]{:S(2)}, u32[]{:S(2)}) %collective-permute-start) | collective-permute-done | bytes 1048608 | tf_op jit(solution)/shard_map/while/body/eval_jaxpr/ppermute | solution.py:17
  439.9 25.6 %convert_bitcast_fusion = bf16[8,1024,256]{1,2,0:T(8,128)(2,1)S(1)} fusion(f32[8,1024,256]{2,1,0:T(8,128)} %get-tuple-element.72, f32[8,1024,256]{2,1,0:T(8,128)} %get-tuple-element.73, f32[1024,256]{1,0:T(8,128)S(1)} %get-tuple-element.76, s32[1024]{0:T(1024)S(1)} %multiply_add_fusion.1, pred[1024]{0:T(1024)(128)(4,1)S(1)} %iota_compare_fusion.1), kind=kOutput, calls=%fused_computation.27 | convolution fusion | flops 4322230272 | bytes 22025216 | tf_op jit(solution)/shard_map/kr,fkc->frc/dot_general | solution.py:97
  466.6 85.2 %all_to_all.23 = bf16[4,8,256,256]{2,3,1,0:T(8,128)(2,1)S(1)} all-to-all(bf16[4,8,256,256]{2,3,1,0:T(8,128)(2,1)S(1)} %pad_maximum_fusion.3), channel_id=1, replica_groups=mesh['grp'=2,'tm'=4,'tile'=4] {'tile'}, dimensions={0} | all-to-all | bytes 8388608 | tf_op jit(solution)/shard_map/all_to_all | solution.py:7
  552.3 20.8 %convolution_convert_fusion = bf16[8,256,1024]{2,1,0:T(8,128)(2,1)} fusion(bf16[8,256,1024]{1,2,0:T(8,128)(2,1)S(1)} %bitcast.45, s32[1024]{0:T(1024)S(1)} %multiply_add_fusion.1, pred[1024]{0:T(1024)(128)(4,1)S(1)} %iota_compare_fusion.1), kind=kOutput, calls=%fused_computation.36 | convolution fusion | flops 4315938816 | bytes 8393728 | tf_op jit(solution)/shard_map/frk,kw->frw/dot_general | solution.py:94
  (63 shorter events, 88.0 us)
Async XLA Ops:
  0.0 108.8 %copy-start.2 = (f32[48]{0:T(128)S(1)}, f32[48]{0:T(128)}, u32[]{:S(2)}) copy-start(f32[48]{0:T(128)} %param.9) | copy-start | bytes 580
  4.5 149.6 %copy-start = (bf16[8,256,1024]{2,0,1:T(8,128)(2,1)}, bf16[8,256,1024]{2,0,1:T(8,128)(2,1)S(1)}, u32[]{:S(2)}) copy-start(bf16[8,256,1024]{2,0,1:T(8,128)(2,1)S(1)} %copy.22) | copy-start | bytes 12582916
  4.5 50.0 %collective-permute-start.1 = (bf16[8,256,1024]{2,0,1:T(8,128)(2,1)S(1)}, bf16[8,256,1024]{2,0,1:T(8,128)(2,1)S(1)}, u32[]{:S(2)}, u32[]{:S(2)}) collective-permute-start(bf16[8,256,1024]{2,0,1:T(8,128)(2,1)S(1)} %copy.22), channel_id=1, source_target_pairs={{0,4},{4,8},{8,12},{1,5},{5,9},{9,13},{2,6},{6,10},{10,14},{3,7},{... | collective-permute-start | bytes 12582920 | tf_op jit(solution)/shard_map/ppermute | solution.py:17
  54.5 49.8 %collective-permute-start.2 = (bf16[8,256,1024]{2,0,1:T(8,128)(2,1)S(1)}, bf16[8,256,1024]{2,0,1:T(8,128)(2,1)S(1)}, u32[]{:S(2)}, u32[]{:S(2)}) collective-permute-start(bf16[8,256,1024]{2,0,1:T(8,128)(2,1)S(1)} %collective-permute-done.1), channel_id=1, source_target_pairs={{0,4},{4,8},{8,12},{1,5},{5,9},{9,13},{2,6},{6,10},{10,14},{3,7},{... | collective-permute-start | bytes 12582920 | tf_op jit(solution)/shard_map/ppermute | solution.py:17
  104.3 49.8 %collective-permute-start.3 = (bf16[8,256,1024]{2,0,1:T(8,128)(2,1)S(1)}, bf16[8,256,1024]{2,0,1:T(8,128)(2,1)S(1)}, u32[]{:S(2)}, u32[]{:S(2)}) collective-permute-start(bf16[8,256,1024]{2,0,1:T(8,128)(2,1)S(1)} %collective-permute-done.2), channel_id=1, source_target_pairs={{0,4},{4,8},{8,12},{1,5},{5,9},{9,13},{2,6},{6,10},{10,14},{3,7},{... | collective-permute-start | bytes 12582920 | tf_op jit(solution)/shard_map/ppermute | solution.py:17
  221.1 5.0 copy-start.1
  221.1 58.3 %all-to-all-start = ((bf16[8,256,1024]{1,0,2:T(8,128)(2,1)}), bf16[8,256,1024]{1,0,2:T(8,128)(2,1)}, u32[]{:S(2)}, u32[]{:S(2)}) async-start(bf16[8,256,1024]{1,0,2:T(8,128)(2,1)} %copy.25), calls=%async_computation | async-start | bytes 8388608 | tf_op jit(solution)/shard_map/all_to_all | solution.py:62
  294.7 23.8 %copy-start.3 = (f32[8]{0:T(128)S(1)}, f32[8]{0:T(128)}, u32[]{:S(2)}) copy-start(f32[8]{0:T(128)} %param.11) | copy-start | bytes 100
  388.8 16.0 %collective-permute-start = (f32[1024,256]{1,0:T(8,128)}, f32[1024,256]{1,0:T(8,128)S(1)}, u32[]{:S(2)}, u32[]{:S(2)}) collective-permute-start(f32[1024,256]{1,0:T(8,128)} %multiply_add_fusion.3), channel_id=1, source_target_pairs={{0,4},{4,8},{8,12},{1,5},{5,9},{9,13},{2,6},{6,10},{10,14},{3,7},{... | collective-permute-start | bytes 3145736 | tf_op jit(solution)/shard_map/while/body/eval_jaxpr/ppermute | solution.py:17
  405.9 16.3 %collective-permute-start = (f32[1024,256]{1,0:T(8,128)}, f32[1024,256]{1,0:T(8,128)S(1)}, u32[]{:S(2)}, u32[]{:S(2)}) collective-permute-start(f32[1024,256]{1,0:T(8,128)} %multiply_add_fusion.3), channel_id=1, source_target_pairs={{0,4},{4,8},{8,12},{1,5},{5,9},{9,13},{2,6},{6,10},{10,14},{3,7},{... | collective-permute-start | bytes 3145736 | tf_op jit(solution)/shard_map/while/body/eval_jaxpr/ppermute | solution.py:17
  423.4 16.3 %collective-permute-start = (f32[1024,256]{1,0:T(8,128)}, f32[1024,256]{1,0:T(8,128)S(1)}, u32[]{:S(2)}, u32[]{:S(2)}) collective-permute-start(f32[1024,256]{1,0:T(8,128)} %multiply_add_fusion.3), channel_id=1, source_target_pairs={{0,4},{4,8},{8,12},{1,5},{5,9},{9,13},{2,6},{6,10},{10,14},{3,7},{... | collective-permute-start | bytes 3145736 | tf_op jit(solution)/shard_map/while/body/eval_jaxpr/ppermute | solution.py:17
